TPU v7x, 32 devices: a whole 2x2x4 slice. The times are simulated.
32 devices in a mesh: tm: 4 (over x, core), pair: 8 (over z, y).
Axes of the slice: x: 2, y: 2, z: 4, core: 2. Of those that a mesh axis runs over, the one named last changes fastest.
Arguments:
- orbitals: bfloat16 [8192, 512], P('pair', 'tm'), may hold values from -1.5 to 1.5
- level_gap: float32 [512], replicated, may hold values from 0.05 to 1.5
- screened: bfloat16 [8, 32, 1024, 1024], P('tm', 'pair'), may hold values from -0.008972168 to 0.008972168
- pair_blocks: int32 [32, 2], P('pair'), may hold values from 0 to 7, as said below
Outputs:
- self_energy: float32 [8, 512, 512], P('tm', 'pair')
Inputs may be any that keep to these rules, and one draw needn't show every extreme that they name: `pair_blocks`: each row names two point blocks a <= c; no unordered pair appears in two rows; the pair (0, 7) appears in every draw.
All inputs are finite; a program needn't handle non-finite values.
Results may differ from a plain program's by a relative error of at most 0.0049.
Values may be sent and summed in bfloat16 or wider, within the bound.
A program may use at most 128 MiB of HBM per device.

v0:
```python
import jax
import jax.numpy as jnp
from jax import lax
from jax.sharding import PartitionSpec as P

NOCC = 128


def shards(orbitals, level_gap, screened, pair_blocks):
    block_rows = orbitals.shape[0]
    wanted = pair_blocks.reshape(-1)
    narrow = lax.all_gather(orbitals, "pair", axis=0, tiled=True)
    picked = jnp.take(narrow.reshape(-1, block_rows, narrow.shape[1]), wanted, axis=0)
    chosen = lax.all_gather(picked, "tm", axis=2, tiled=True)
    orbital_count = chosen.shape[2]
    time_local = screened.shape[0]
    pair_local = screened.shape[1]
    time_total = time_local * lax.axis_size("tm")
    first_time = lax.axis_index("tm") * time_local
    moments = (first_time + jnp.arange(time_local)).astype(jnp.float32)
    tau = 6.0 * (moments + 0.5) / time_total
    signs = jnp.where(jnp.arange(orbital_count) < NOCC, 1.0, -1.0).astype(jnp.float32)
    factors = signs[None, :] * jnp.exp(-level_gap[None, :] * tau[:, None])
    totals = []
    for time_step in range(time_local):
        total = jnp.zeros((orbital_count, orbital_count), jnp.float32)
        for pair_step in range(pair_local):
            left = chosen[2 * pair_step]
            right = chosen[2 * pair_step + 1]
            scaled = (left.astype(jnp.float32) * factors[time_step][None, :]).astype(jnp.bfloat16)
            green = lax.dot_general(
                scaled, right, (((1,), (1,)), ((), ())), preferred_element_type=jnp.float32
            )
            product = (green * screened[time_step, pair_step].astype(jnp.float32)).astype(
                jnp.bfloat16
            )
            half = lax.dot_general(
                left, product, (((0,), (0,)), ((), ())), preferred_element_type=jnp.float32
            ).astype(jnp.bfloat16)
            block = jnp.dot(half, right, preferred_element_type=jnp.float32)
            weight = jnp.where(
                pair_blocks[pair_step, 0] == pair_blocks[pair_step, 1], 0.5, 1.0
            ).astype(jnp.float32)
            total = total + weight * (block + block.T)
        totals.append(total)
    partial_sum = jnp.stack(totals, axis=0)
    return lax.psum_scatter(partial_sum, "pair", scatter_dimension=1, tiled=True)


def solution(mesh):
    return jax.shard_map(
        shards,
        mesh=mesh,
        in_specs=(P("pair", "tm"), P(), P("tm", "pair", None, None), P("pair", None)),
        out_specs=P("tm", "pair", None),
        check_vma=False,
    )
```

profile of v0, /device:TPU:0, one launch (start us, length us, event | category | flops | bytes accessed | tf_op | source)
XLA Modules:
  0.0 293.7 jit_solution(13461157398110118424)
XLA Ops:
  8.3 53.0 %all-gather.3.cloned.1.call-done = bf16[8192,128]{1,0:T(8,128)(2,1)} async-done(((bf16[1024,128]{1,0:T(8,128)(2,1)}), bf16[8192,128]{1,0:T(8,128)(2,1)}) %all-gather.3.cloned.1.call-update) | async-done | bytes 2097168 | tf_op jit(solution)/shard_map/all_gather | solution.py:12
  61.3 2.5 gather_fusion
  71.4 52.2 %all-gather.5.cloned.1.call-done = bf16[8,1024,512]{2,1,0:T(8,128)(2,1)} async-done(((bf16[8,1024,128]{2,1,0:T(8,128)(2,1)}), bf16[8,1024,512]{2,1,0:T(8,128)(2,1)}) %all-gather.5.cloned.1.call-update) | async-done | bytes 8388624 | tf_op jit(solution)/shard_map/all_gather | solution.py:14
  123.6 4.9 %convolution_convert_fusion.3 = bf16[512,1024]{1,0:T(8,128)(2,1)S(1)} fusion(bf16[2,4,1024,1024]{3,2,1,0:T(8,128)(2,1)} %param.6, f32[512]{0:T(512)S(1)} %bitcast.218, bf16[8,1024,512]{2,1,0:T(8,128)(2,1)} %all-gather.5.cloned.1.call-done), kind=kOutput, calls=%fused_computation.38 | convolution fusion | flops 2152726528 | bytes 6293504 | tf_op jit(solution)/shard_map/dot_general | solution.py:37
  130.8 6.0 %convolution_convert_fusion.2 = bf16[512,1024]{1,0:T(8,128)(2,1)} fusion(bf16[2,4,1024,1024]{3,2,1,0:T(8,128)(2,1)} %param.6, f32[512]{0:T(512)S(1)} %bitcast.219, bf16[8,1024,512]{2,1,0:T(8,128)(2,1)} %all-gather.5.cloned.1.call-done), kind=kOutput, calls=%fused_computation.37 | convolution fusion | flops 2152726528 | bytes 6293504 | tf_op jit(solution)/shard_map/dot_general | solution.py:37
  140.4 5.9 %convolution_convert_fusion = bf16[512,1024]{1,0:T(8,128)(2,1)} fusion(bf16[2,4,1024,1024]{3,2,1,0:T(8,128)(2,1)} %param.6, f32[512]{0:T(512)S(1)} %bitcast.220, bf16[8,1024,512]{2,1,0:T(8,128)(2,1)} %all-gather.5.cloned.1.call-done), kind=kOutput, calls=%fused_computation.35 | convolution fusion | flops 2152726528 | bytes 6293504 | tf_op jit(solution)/shard_map/dot_general | solution.py:37
  146.3 3.2 %fusion.110 = f32[512,512]{1,0:T(8,128)} fusion(bf16[512,1024]{1,0:T(8,128)(2,1)} %convolution_convert_fusion, bf16[8,1024,512]{2,1,0:T(8,128)(2,1)} %all-gather.5.cloned.1.call-done), kind=kOutput, calls=%fused_computation.109 | convolution fusion | flops 536870912 | bytes 3145728 | tf_op jit(solution)/shard_map/dot_general | solution.py:40
  149.6 2.5 copy.24
  152.1 6.0 %convolution_convert_fusion.1 = bf16[512,1024]{1,0:T(8,128)(2,1)} fusion(bf16[2,4,1024,1024]{3,2,1,0:T(8,128)(2,1)} %param.6, f32[512]{0:T(512)S(1)} %bitcast.221, bf16[8,1024,512]{2,1,0:T(8,128)(2,1)} %all-gather.5.cloned.1.call-done), kind=kOutput, calls=%fused_computation.36 | convolution fusion | flops 2152726528 | bytes 6293504 | tf_op jit(solution)/shard_map/dot_general | solution.py:37
  158.1 3.2 %fusion.108 = f32[512,512]{1,0:T(8,128)} fusion(bf16[512,1024]{1,0:T(8,128)(2,1)} %convolution_convert_fusion.1, bf16[8,1024,512]{2,1,0:T(8,128)(2,1)} %all-gather.5.cloned.1.call-done), kind=kOutput, calls=%fused_computation.107 | convolution fusion | flops 536870912 | bytes 3145728 | tf_op jit(solution)/shard_map/dot_general | solution.py:40
  161.3 2.6 copy.23
  163.9 6.1 %convolution_convert_fusion.4 = bf16[512,1024]{1,0:T(8,128)(2,1)} fusion(bf16[2,4,1024,1024]{3,2,1,0:T(8,128)(2,1)} %param.6, f32[512]{0:T(512)S(1)} %bitcast.214, bf16[8,1024,512]{2,1,0:T(8,128)(2,1)} %all-gather.5.cloned.1.call-done), kind=kOutput, calls=%fused_computation.39 | convolution fusion | flops 2152726528 | bytes 6293504 | tf_op jit(solution)/shard_map/dot_general | solution.py:37
  170.0 3.2 %fusion.111 = f32[512,512]{1,0:T(8,128)} fusion(bf16[512,1024]{1,0:T(8,128)(2,1)} %convolution_convert_fusion.4, bf16[8,1024,512]{2,1,0:T(8,128)(2,1)} %all-gather.5.cloned.1.call-done), kind=kOutput, calls=%fused_computation.110 | convolution fusion | flops 536870912 | bytes 3145728 | tf_op jit(solution)/shard_map/dot_general | solution.py:40
  173.2 2.5 copy.20
  175.7 5.9 %convolution_convert_fusion.5 = bf16[512,1024]{1,0:T(8,128)(2,1)} fusion(bf16[2,4,1024,1024]{3,2,1,0:T(8,128)(2,1)} %param.6, f32[512]{0:T(512)S(1)} %bitcast.215, bf16[8,1024,512]{2,1,0:T(8,128)(2,1)} %all-gather.5.cloned.1.call-done), kind=kOutput, calls=%fused_computation.40 | convolution fusion | flops 2152726528 | bytes 6293504 | tf_op jit(solution)/shard_map/dot_general | solution.py:37
  181.7 3.2 %fusion.109 = f32[512,512]{1,0:T(8,128)} fusion(bf16[512,1024]{1,0:T(8,128)(2,1)} %convolution_convert_fusion.5, bf16[8,1024,512]{2,1,0:T(8,128)(2,1)} %all-gather.5.cloned.1.call-done), kind=kOutput, calls=%fused_computation.108 | convolution fusion | flops 536870912 | bytes 3145728 | tf_op jit(solution)/shard_map/dot_general | solution.py:40
  184.9 2.5 copy.19
  187.4 5.9 %convolution_convert_fusion.7 = bf16[512,1024]{1,0:T(8,128)(2,1)} fusion(bf16[2,4,1024,1024]{3,2,1,0:T(8,128)(2,1)} %param.6, f32[512]{0:T(512)S(1)} %bitcast.216, bf16[8,1024,512]{2,1,0:T(8,128)(2,1)} %all-gather.5.cloned.1.call-done), kind=kOutput, calls=%fused_computation.42 | convolution fusion | flops 2152726528 | bytes 6293504 | tf_op jit(solution)/shard_map/dot_general | solution.py:37
  193.3 3.2 %fusion.105 = f32[512,512]{1,0:T(8,128)} fusion(bf16[512,1024]{1,0:T(8,128)(2,1)} %convolution_convert_fusion.7, bf16[8,1024,512]{2,1,0:T(8,128)(2,1)} %all-gather.5.cloned.1.call-done), kind=kOutput, calls=%fused_computation.104 | convolution fusion | flops 536870912 | bytes 3145728 | tf_op jit(solution)/shard_map/dot_general | solution.py:40
  199.1 5.9 %convolution_convert_fusion.6 = bf16[512,1024]{1,0:T(8,128)(2,1)} fusion(bf16[2,4,1024,1024]{3,2,1,0:T(8,128)(2,1)} %param.6, f32[512]{0:T(512)S(1)} %bitcast.217, bf16[8,1024,512]{2,1,0:T(8,128)(2,1)} %all-gather.5.cloned.1.call-done), kind=kOutput, calls=%fused_computation.41 | convolution fusion | flops 2152726528 | bytes 6293504 | tf_op jit(solution)/shard_map/dot_general | solution.py:37
  205.0 3.3 %fusion.107 = f32[512,512]{1,0:T(8,128)} fusion(bf16[512,1024]{1,0:T(8,128)(2,1)} %convolution_convert_fusion.6, bf16[8,1024,512]{2,1,0:T(8,128)(2,1)} %all-gather.5.cloned.1.call-done), kind=kOutput, calls=%fused_computation.106 | convolution fusion | flops 536870912 | bytes 3145728 | tf_op jit(solution)/shard_map/dot_general | solution.py:40
  208.3 2.5 copy.18
  210.8 3.7 %fusion.34 = f32[1,512,512]{2,1,0:T(8,128)S(1)} fusion(f32[512,512]{1,0:T(8,128)} %fusion.110, f32[512,512]{0,1:T(8,128)} %copy.24, f32[512,512]{1,0:T(8,128)} %fusion.108, f32[512,512]{0,1:T(8,128)} %copy.23, f32[512,512]{1,0:T(8,128)S(1)} %fusion.106, f32[512,512]{0,1:T(8,128)} %copy.22, f32[512,512]{1,0:T(8,128)S(1)} %fusion.104, ...), kind=kLoop, calls=%fused_computation.58 | loop fusion | flops 2883584 | bytes 9437200 | tf_op jit(solution)/shard_map/stack | solution.py:46
  218.3 68.9 %reduce-scatter.2.cloned.1.call-done = f32[2,64,512]{2,1,0:T(8,128)} async-done(((f32[2,512,512]{2,1,0:T(8,128)}), f32[2,64,512]{2,1,0:T(8,128)}) %reduce-scatter.2.cloned.1.call-update) | async-done | bytes 262160 | tf_op jit(solution)/shard_map/reduce_scatter | solution.py:47
  (46 shorter events, 16.4 us)
Async XLA Ops:
  6.5 54.8 %all-gather.3.cloned.1.call-start = ((), (), s32[]{:S(2)}) async-start(), calls=%async_computation.1 | async-start | bytes 2359296 | tf_op jit(solution)/shard_map/all_gather | solution.py:12
  7.3 116.4 %all-gather.5.cloned.1.call-start = ((), (), s32[]{:S(2)}) async-start(), calls=%async_computation.2 | async-start | bytes 10485760 | tf_op jit(solution)/shard_map/all_gather | solution.py:14
  63.8 1.8 copy-start.9
  63.9 1.8 copy-start.8
  65.5 221.7 %reduce-scatter.2.cloned.1.call-start = ((), (), s32[]{:S(2)}) async-start(), calls=%async_computation.3 | async-start | bytes 2359296 | tf_op jit(solution)/shard_map/reduce_scatter | solution.py:47
  210.8 3.8 %copy-start = (f32[512,512]{1,0:T(8,128)S(1)}, f32[512,512]{1,0:T(8,128)}, u32[]{:S(2)}) copy-start(f32[512,512]{1,0:T(8,128)} %fusion.111) | copy-start | bytes 3145732
  210.8 3.8 %copy-start.1 = (f32[512,512]{0,1:T(8,128)S(1)}, f32[512,512]{0,1:T(8,128)}, u32[]{:S(2)}) copy-start(f32[512,512]{0,1:T(8,128)} %copy.20) | copy-start | bytes 3145732
  210.8 3.8 %copy-start.2 = (f32[512,512]{1,0:T(8,128)S(1)}, f32[512,512]{1,0:T(8,128)}, u32[]{:S(2)}) copy-start(f32[512,512]{1,0:T(8,128)} %fusion.109) | copy-start | bytes 3145732
  210.8 3.8 %copy-start.3 = (f32[512,512]{0,1:T(8,128)S(1)}, f32[512,512]{0,1:T(8,128)}, u32[]{:S(2)}) copy-start(f32[512,512]{0,1:T(8,128)} %copy.19) | copy-start | bytes 3145732
  210.8 4.1 %copy-start.4 = (f32[512,512]{1,0:T(8,128)S(1)}, f32[512,512]{1,0:T(8,128)}, u32[]{:S(2)}) copy-start(f32[512,512]{1,0:T(8,128)} %fusion.105) | copy-start | bytes 3145732
  210.8 4.4 %copy-start.5 = (f32[512,512]{0,1:T(8,128)S(1)}, f32[512,512]{0,1:T(8,128)}, u32[]{:S(2)}) copy-start(f32[512,512]{0,1:T(8,128)} %copy.17) | copy-start | bytes 3145732
  210.8 4.7 %copy-start.6 = (f32[512,512]{1,0:T(8,128)S(1)}, f32[512,512]{1,0:T(8,128)}, u32[]{:S(2)}) copy-start(f32[512,512]{1,0:T(8,128)} %fusion.107) | copy-start | bytes 3145732
  210.8 4.9 %copy-start.7 = (f32[512,512]{0,1:T(8,128)S(1)}, f32[512,512]{0,1:T(8,128)}, u32[]{:S(2)}) copy-start(f32[512,512]{0,1:T(8,128)} %copy.18) | copy-start | bytes 3145732
Sparse Core Ops, SparseCore 0:
  9.5 51.7 all-gather.2
  65.7 57.8 all-gather.4
  218.5 68.6 reduce-scatter.1
where the time goes:
time: 294 us
  waiting for transfers between devices  175 us (60%)
  matrix products  70.1 us (24%)
  local copies, waits for them, and re-layouts  22.4 us (8%)
  between operations  18.3 us (6%)
  other arithmetic  8.04 us (3%)
    reduce_scatter x1, waiting for transfers between devices, shards(): lax.psum_scatter(partial_sum, 'pair', scatter_dimension=1, tiled=True)  68.9 us
    all_gather x1, waiting for transfers between devices, shards(): narrow = lax.all_gather(orbitals, 'pair', axis=0, tiled=True)  53 us
    all_gather x1, waiting for transfers between devices, shards(): chosen = lax.all_gather(picked, 'tm', axis=2, tiled=True)  52.2 us
    dot_general x8, matrix products, shards(): lax.dot_general(left, product, (((0,), (0,)), ((), ())), preferred_elemen...  46.5 us
    dot_general x8, matrix products, shards(): block = jnp.dot(half, right, preferred_element_type=jnp.float32)  23.6 us
    dot_general x8, local copies, waits for them, and re-layouts, shards(): block = jnp.dot(half, right, preferred_element_type=jnp.float32)  17 us
    another operation x3, other arithmetic, shards(): partial_sum = jnp.stack(totals, axis=0)  6.27 us
  transfers between devices with their start and end apart: 3, of which 3 were waited for; matrix products, arithmetic and copies ran while one was open for 1% of the time, Pallas kernels for 0%

commit v1 on v0

--- a/solution.py
+++ b/solution.py
@@ -9,7 +9,13 @@
 def shards(orbitals, level_gap, screened, pair_blocks):
     block_rows = orbitals.shape[0]
     wanted = pair_blocks.reshape(-1)
-    narrow = lax.all_gather(orbitals, "pair", axis=0, tiled=True)
+    devices = lax.axis_size("pair")
+    moving, shards_2 = (orbitals, [orbitals])
+    for _ in range(devices - 1):
+        moving = lax.ppermute(moving, "pair", [(i, (i + 1) % devices) for i in range(devices)])
+        shards_2.insert(0, moving)
+    line = jnp.concatenate(shards_2, axis=0)
+    narrow = jnp.roll(line, (lax.axis_index("pair") + 1) * orbitals.shape[0], axis=0)
     picked = jnp.take(narrow.reshape(-1, block_rows, narrow.shape[1]), wanted, axis=0)
     chosen = lax.all_gather(picked, "tm", axis=2, tiled=True)
     orbital_count = chosen.shape[2]

time: 294 us -> 311 us (1.058)
  waiting for transfers between devices: 175 us -> 185 us
  starting transfers between devices: 0.08 us -> 3.24 us
    ppermute x0 -> x7, waiting for transfers between devices: none -> 65 us  [shards(): lax.ppermute(moving, 'pair', [(i, (i + 1) % devices) for i in range(devic...]
    all_gather x1 -> x0, waiting for transfers between devices: 53 us -> none  [shards(): narrow = lax.all_gather(orbitals, 'pair', axis=0, tiled=True)]
  transfers between devices with their start and end apart: 3 -> 9, of which waited for: 3 -> 9; matrix products, arithmetic and copies ran while one was open for 1% -> 1% of each run, Pallas kernels for 0% -> 0%
where the time goes in v1:
time: 311 us; the launch traced here: 310 us
  waiting for transfers between devices  185 us (59%)
  matrix products  70.2 us (23%)
  local copies, waits for them, and re-layouts  23.7 us (8%)
  between operations  18.8 us (6%)
  other arithmetic  9.65 us (3%)
  starting transfers between devices  3.24 us (1%)
    reduce_scatter x1, waiting for transfers between devices, shards(): lax.psum_scatter(partial_sum, 'pair', scatter_dimension=1, tiled=True)  68.9 us
    ppermute x7, waiting for transfers between devices, shards(): lax.ppermute(moving, 'pair', [(i, (i + 1) % devices) for i in range(devic...  65 us
    all_gather x1, waiting for transfers between devices, shards(): chosen = lax.all_gather(picked, 'tm', axis=2, tiled=True)  50.6 us
    dot_general x8, matrix products, shards(): lax.dot_general(left, product, (((0,), (0,)), ((), ())), preferred_elemen...  46.6 us
    dot_general x8, matrix products, shards(): block = jnp.dot(half, right, preferred_element_type=jnp.float32)  23.5 us
    dot_general x8, local copies, waits for them, and re-layouts, shards(): block = jnp.dot(half, right, preferred_element_type=jnp.float32)  17.1 us
    another operation x3, other arithmetic, shards(): partial_sum = jnp.stack(totals, axis=0)  6.26 us
  transfers between devices with their start and end apart: 9, of which 9 were waited for; matrix products, arithmetic and copies ran while one was open for 1% of the time, Pallas kernels for 0%

profile of v1, /device:TPU:0, one launch (start us, length us, event | category | flops | bytes accessed | tf_op | source)
XLA Modules:
  0.0 310.1 jit_solution(5586169564269264432)
XLA Ops:
  9.5 9.6 %collective-permute-done = bf16[1024,128]{1,0:T(8,128)(2,1)S(1)} collective-permute-done((bf16[1024,128]{1,0:T(8,128)(2,1)}, bf16[1024,128]{1,0:T(8,128)(2,1)S(1)}, u32[]{:S(2)}, u32[]{:S(2)}) %collective-permute-start) | collective-permute-done | bytes 262176 | tf_op jit(solution)/shard_map/ppermute | solution.py:15
  19.2 10.2 %collective-permute-done.1 = bf16[1024,128]{1,0:T(8,128)(2,1)S(1)} collective-permute-done((bf16[1024,128]{1,0:T(8,128)(2,1)S(1)}, bf16[1024,128]{1,0:T(8,128)(2,1)S(1)}, u32[]{:S(2)}, u32[]{:S(2)}) %collective-permute-start.1) | collective-permute-done | bytes 262176 | tf_op jit(solution)/shard_map/ppermute | solution.py:15
  29.3 9.3 %collective-permute-done.2 = bf16[1024,128]{1,0:T(8,128)(2,1)S(1)} collective-permute-done((bf16[1024,128]{1,0:T(8,128)(2,1)S(1)}, bf16[1024,128]{1,0:T(8,128)(2,1)S(1)}, u32[]{:S(2)}, u32[]{:S(2)}) %collective-permute-start.2) | collective-permute-done | bytes 262176 | tf_op jit(solution)/shard_map/ppermute | solution.py:15
  38.6 9.1 %collective-permute-done.3 = bf16[1024,128]{1,0:T(8,128)(2,1)S(1)} collective-permute-done((bf16[1024,128]{1,0:T(8,128)(2,1)S(1)}, bf16[1024,128]{1,0:T(8,128)(2,1)S(1)}, u32[]{:S(2)}, u32[]{:S(2)}) %collective-permute-start.3) | collective-permute-done | bytes 262176 | tf_op jit(solution)/shard_map/ppermute | solution.py:15
  47.7 9.1 %collective-permute-done.4 = bf16[1024,128]{1,0:T(8,128)(2,1)S(1)} collective-permute-done((bf16[1024,128]{1,0:T(8,128)(2,1)S(1)}, bf16[1024,128]{1,0:T(8,128)(2,1)S(1)}, u32[]{:S(2)}, u32[]{:S(2)}) %collective-permute-start.4) | collective-permute-done | bytes 262176 | tf_op jit(solution)/shard_map/ppermute | solution.py:15
  57.6 8.8 %collective-permute-done.5 = bf16[1024,128]{1,0:T(8,128)(2,1)S(1)} collective-permute-done((bf16[1024,128]{1,0:T(8,128)(2,1)S(1)}, bf16[1024,128]{1,0:T(8,128)(2,1)S(1)}, u32[]{:S(2)}, u32[]{:S(2)}) %collective-permute-start.5) | collective-permute-done | bytes 262176 | tf_op jit(solution)/shard_map/ppermute | solution.py:15
  66.6 9.0 %collective-permute-done.6 = bf16[1024,128]{1,0:T(8,128)(2,1)S(1)} collective-permute-done((bf16[1024,128]{1,0:T(8,128)(2,1)S(1)}, bf16[1024,128]{1,0:T(8,128)(2,1)S(1)}, u32[]{:S(2)}, u32[]{:S(2)}) %collective-permute-start.6) | collective-permute-done | bytes 262176 | tf_op jit(solution)/shard_map/ppermute | solution.py:15
  79.5 3.3 %broadcast_select_fusion = bf16[8,1024,128]{2,1,0:T(8,128)(2,1)} fusion(bf16[8,1024,128]{2,1,0:T(8,128)(2,1)} %gather_fusion, pred[8]{0:T(512)(128)(4,1)S(1)} %compare_and_fusion), kind=kLoop, calls=%fused_computation.34 | loop fusion | flops 1048576 | bytes 4194312 | tf_op jit(solution)/shard_map/jit(_take)/select_n | solution.py:19
  88.9 50.6 %all-gather.2.cloned.1.call-done = bf16[8,1024,512]{2,1,0:T(8,128)(2,1)} async-done(((bf16[8,1024,128]{2,1,0:T(8,128)(2,1)}), bf16[8,1024,512]{2,1,0:T(8,128)(2,1)}) %all-gather.2.cloned.1.call-update) | async-done | bytes 8388624 | tf_op jit(solution)/shard_map/all_gather | solution.py:20
  139.5 4.9 %convolution_convert_fusion.3 = bf16[512,1024]{1,0:T(8,128)(2,1)S(1)} fusion(bf16[2,4,1024,1024]{3,2,1,0:T(8,128)(2,1)} %param.6, f32[512]{0:T(512)S(1)} %bitcast.218, bf16[8,1024,512]{2,1,0:T(8,128)(2,1)} %all-gather.2.cloned.1.call-done), kind=kOutput, calls=%fused_computation.38 | convolution fusion | flops 2152726528 | bytes 6293504 | tf_op jit(solution)/shard_map/dot_general | solution.py:43
  146.7 6.0 %convolution_convert_fusion.2 = bf16[512,1024]{1,0:T(8,128)(2,1)} fusion(bf16[2,4,1024,1024]{3,2,1,0:T(8,128)(2,1)} %param.6, f32[512]{0:T(512)S(1)} %bitcast.219, bf16[8,1024,512]{2,1,0:T(8,128)(2,1)} %all-gather.2.cloned.1.call-done), kind=kOutput, calls=%fused_computation.37 | convolution fusion | flops 2152726528 | bytes 6293504 | tf_op jit(solution)/shard_map/dot_general | solution.py:43
  156.3 5.9 %convolution_convert_fusion = bf16[512,1024]{1,0:T(8,128)(2,1)} fusion(bf16[2,4,1024,1024]{3,2,1,0:T(8,128)(2,1)} %param.6, f32[512]{0:T(512)S(1)} %bitcast.220, bf16[8,1024,512]{2,1,0:T(8,128)(2,1)} %all-gather.2.cloned.1.call-done), kind=kOutput, calls=%fused_computation.35 | convolution fusion | flops 2152726528 | bytes 6293504 | tf_op jit(solution)/shard_map/dot_general | solution.py:43
  162.2 3.3 %fusion.110 = f32[512,512]{1,0:T(8,128)} fusion(bf16[512,1024]{1,0:T(8,128)(2,1)} %convolution_convert_fusion, bf16[8,1024,512]{2,1,0:T(8,128)(2,1)} %all-gather.2.cloned.1.call-done), kind=kOutput, calls=%fused_computation.109 | convolution fusion | flops 536870912 | bytes 3145728 | tf_op jit(solution)/shard_map/dot_general | solution.py:46
  168.0 6.0 %convolution_convert_fusion.1 = bf16[512,1024]{1,0:T(8,128)(2,1)} fusion(bf16[2,4,1024,1024]{3,2,1,0:T(8,128)(2,1)} %param.6, f32[512]{0:T(512)S(1)} %bitcast.221, bf16[8,1024,512]{2,1,0:T(8,128)(2,1)} %all-gather.2.cloned.1.call-done), kind=kOutput, calls=%fused_computation.36 | convolution fusion | flops 2152726528 | bytes 6293504 | tf_op jit(solution)/shard_map/dot_general | solution.py:43
  174.0 3.2 %fusion.108 = f32[512,512]{1,0:T(8,128)} fusion(bf16[512,1024]{1,0:T(8,128)(2,1)} %convolution_convert_fusion.1, bf16[8,1024,512]{2,1,0:T(8,128)(2,1)} %all-gather.2.cloned.1.call-done), kind=kOutput, calls=%fused_computation.107 | convolution fusion | flops 536870912 | bytes 3145728 | tf_op jit(solution)/shard_map/dot_general | solution.py:46
  179.8 6.1 %convolution_convert_fusion.4 = bf16[512,1024]{1,0:T(8,128)(2,1)} fusion(bf16[2,4,1024,1024]{3,2,1,0:T(8,128)(2,1)} %param.6, f32[512]{0:T(512)S(1)} %bitcast.214, bf16[8,1024,512]{2,1,0:T(8,128)(2,1)} %all-gather.2.cloned.1.call-done), kind=kOutput, calls=%fused_computation.39 | convolution fusion | flops 2152726528 | bytes 6293504 | tf_op jit(solution)/shard_map/dot_general | solution.py:43
  186.0 3.2 %fusion.111 = f32[512,512]{1,0:T(8,128)} fusion(bf16[512,1024]{1,0:T(8,128)(2,1)} %convolution_convert_fusion.4, bf16[8,1024,512]{2,1,0:T(8,128)(2,1)} %all-gather.2.cloned.1.call-done), kind=kOutput, calls=%fused_computation.110 | convolution fusion | flops 536870912 | bytes 3145728 | tf_op jit(solution)/shard_map/dot_general | solution.py:46
  191.8 5.9 %convolution_convert_fusion.5 = bf16[512,1024]{1,0:T(8,128)(2,1)} fusion(bf16[2,4,1024,1024]{3,2,1,0:T(8,128)(2,1)} %param.6, f32[512]{0:T(512)S(1)} %bitcast.215, bf16[8,1024,512]{2,1,0:T(8,128)(2,1)} %all-gather.2.cloned.1.call-done), kind=kOutput, calls=%fused_computation.40 | convolution fusion | flops 2152726528 | bytes 6293504 | tf_op jit(solution)/shard_map/dot_general | solution.py:43
  197.7 3.2 %fusion.109 = f32[512,512]{1,0:T(8,128)} fusion(bf16[512,1024]{1,0:T(8,128)(2,1)} %convolution_convert_fusion.5, bf16[8,1024,512]{2,1,0:T(8,128)(2,1)} %all-gather.2.cloned.1.call-done), kind=kOutput, calls=%fused_computation.108 | convolution fusion | flops 536870912 | bytes 3145728 | tf_op jit(solution)/shard_map/dot_general | solution.py:46
  203.5 5.9 %convolution_convert_fusion.7 = bf16[512,1024]{1,0:T(8,128)(2,1)} fusion(bf16[2,4,1024,1024]{3,2,1,0:T(8,128)(2,1)} %param.6, f32[512]{0:T(512)S(1)} %bitcast.216, bf16[8,1024,512]{2,1,0:T(8,128)(2,1)} %all-gather.2.cloned.1.call-done), kind=kOutput, calls=%fused_computation.42 | convolution fusion | flops 2152726528 | bytes 6293504 | tf_op jit(solution)/shard_map/dot_general | solution.py:43
  209.4 3.2 %fusion.105 = f32[512,512]{1,0:T(8,128)} fusion(bf16[512,1024]{1,0:T(8,128)(2,1)} %convolution_convert_fusion.7, bf16[8,1024,512]{2,1,0:T(8,128)(2,1)} %all-gather.2.cloned.1.call-done), kind=kOutput, calls=%fused_computation.104 | convolution fusion | flops 536870912 | bytes 3145728 | tf_op jit(solution)/shard_map/dot_general | solution.py:46
  215.1 5.9 %convolution_convert_fusion.6 = bf16[512,1024]{1,0:T(8,128)(2,1)} fusion(bf16[2,4,1024,1024]{3,2,1,0:T(8,128)(2,1)} %param.6, f32[512]{0:T(512)S(1)} %bitcast.217, bf16[8,1024,512]{2,1,0:T(8,128)(2,1)} %all-gather.2.cloned.1.call-done), kind=kOutput, calls=%fused_computation.41 | convolution fusion | flops 2152726528 | bytes 6293504 | tf_op jit(solution)/shard_map/dot_general | solution.py:43
  226.9 3.7 %fusion.34 = f32[1,512,512]{2,1,0:T(8,128)S(1)} fusion(f32[512,512]{1,0:T(8,128)} %fusion.110, f32[512,512]{0,1:T(8,128)} %copy.24, f32[512,512]{1,0:T(8,128)} %fusion.108, f32[512,512]{0,1:T(8,128)} %copy.23, f32[512,512]{1,0:T(8,128)S(1)} %fusion.106, f32[512,512]{0,1:T(8,128)} %copy.22, f32[512,512]{1,0:T(8,128)S(1)} %fusion.104, ...), kind=kLoop, calls=%fused_computation.58 | loop fusion | flops 2883584 | bytes 9437200 | tf_op jit(solution)/shard_map/stack | solution.py:52
  234.3 68.9 %reduce-scatter.2.cloned.1.call-done = f32[2,64,512]{2,1,0:T(8,128)} async-done(((f32[2,512,512]{2,1,0:T(8,128)}), f32[2,64,512]{2,1,0:T(8,128)}) %reduce-scatter.2.cloned.1.call-update) | async-done | bytes 262160 | tf_op jit(solution)/shard_map/reduce_scatter | solution.py:53
  (76 shorter events, 37.0 us)
Async XLA Ops:
  6.5 70.6 %copy-start.8 = (bf16[1024,128]{1,0:T(8,128)(2,1)S(1)}, bf16[1024,128]{1,0:T(8,128)(2,1)}, u32[]{:S(2)}) copy-start(bf16[1024,128]{1,0:T(8,128)(2,1)} %param.4) | copy-start | bytes 786436
  6.5 133.0 %all-gather.2.cloned.1.call-start = ((), (), s32[]{:S(2)}) async-start(), calls=%async_computation.1 | async-start | bytes 10485760 | tf_op jit(solution)/shard_map/all_gather | solution.py:20
  6.5 12.6 %collective-permute-start = (bf16[1024,128]{1,0:T(8,128)(2,1)}, bf16[1024,128]{1,0:T(8,128)(2,1)S(1)}, u32[]{:S(2)}, u32[]{:S(2)}) collective-permute-start(bf16[1024,128]{1,0:T(8,128)(2,1)} %param.4), channel_id=1, source_target_pairs={{0,1},{1,2},{2,3},{3,4},{4,5},{5,6},{6,7},{7,0},{8,9},{9,10},{10,1... | collective-permute-start | bytes 786440 | tf_op jit(solution)/shard_map/ppermute | solution.py:15
  19.2 10.2 %collective-permute-start.1 = (bf16[1024,128]{1,0:T(8,128)(2,1)S(1)}, bf16[1024,128]{1,0:T(8,128)(2,1)S(1)}, u32[]{:S(2)}, u32[]{:S(2)}) collective-permute-start(bf16[1024,128]{1,0:T(8,128)(2,1)S(1)} %collective-permute-done), channel_id=1, source_target_pairs={{0,1},{1,2},{2,3},{3,4},{4,5},{5,6},{6,7},{7,0},{8,9},{9,10},{10,1... | collective-permute-start | bytes 786440 | tf_op jit(solution)/shard_map/ppermute | solution.py:15
  29.3 9.3 %collective-permute-start.2 = (bf16[1024,128]{1,0:T(8,128)(2,1)S(1)}, bf16[1024,128]{1,0:T(8,128)(2,1)S(1)}, u32[]{:S(2)}, u32[]{:S(2)}) collective-permute-start(bf16[1024,128]{1,0:T(8,128)(2,1)S(1)} %collective-permute-done.1), channel_id=1, source_target_pairs={{0,1},{1,2},{2,3},{3,4},{4,5},{5,6},{6,7},{7,0},{8,9},{9,10},{10,1... | collective-permute-start | bytes 786440 | tf_op jit(solution)/shard_map/ppermute | solution.py:15
  38.6 9.1 %collective-permute-start.3 = (bf16[1024,128]{1,0:T(8,128)(2,1)S(1)}, bf16[1024,128]{1,0:T(8,128)(2,1)S(1)}, u32[]{:S(2)}, u32[]{:S(2)}) collective-permute-start(bf16[1024,128]{1,0:T(8,128)(2,1)S(1)} %collective-permute-done.2), channel_id=1, source_target_pairs={{0,1},{1,2},{2,3},{3,4},{4,5},{5,6},{6,7},{7,0},{8,9},{9,10},{10,1... | collective-permute-start | bytes 786440 | tf_op jit(solution)/shard_map/ppermute | solution.py:15
  47.7 9.1 %collective-permute-start.4 = (bf16[1024,128]{1,0:T(8,128)(2,1)S(1)}, bf16[1024,128]{1,0:T(8,128)(2,1)S(1)}, u32[]{:S(2)}, u32[]{:S(2)}) collective-permute-start(bf16[1024,128]{1,0:T(8,128)(2,1)S(1)} %collective-permute-done.3), channel_id=1, source_target_pairs={{0,1},{1,2},{2,3},{3,4},{4,5},{5,6},{6,7},{7,0},{8,9},{9,10},{10,1... | collective-permute-start | bytes 786440 | tf_op jit(solution)/shard_map/ppermute | solution.py:15
  56.8 9.7 %collective-permute-start.5 = (bf16[1024,128]{1,0:T(8,128)(2,1)S(1)}, bf16[1024,128]{1,0:T(8,128)(2,1)S(1)}, u32[]{:S(2)}, u32[]{:S(2)}) collective-permute-start(bf16[1024,128]{1,0:T(8,128)(2,1)S(1)} %collective-permute-done.4), channel_id=1, source_target_pairs={{0,1},{1,2},{2,3},{3,4},{4,5},{5,6},{6,7},{7,0},{8,9},{9,10},{10,1... | collective-permute-start | bytes 786440 | tf_op jit(solution)/shard_map/ppermute | solution.py:15
  66.5 9.1 %collective-permute-start.6 = (bf16[1024,128]{1,0:T(8,128)(2,1)S(1)}, bf16[1024,128]{1,0:T(8,128)(2,1)S(1)}, u32[]{:S(2)}, u32[]{:S(2)}) collective-permute-start(bf16[1024,128]{1,0:T(8,128)(2,1)S(1)} %collective-permute-done.5), channel_id=1, source_target_pairs={{0,1},{1,2},{2,3},{3,4},{4,5},{5,6},{6,7},{7,0},{8,9},{9,10},{10,1... | collective-permute-start | bytes 786440 | tf_op jit(solution)/shard_map/ppermute | solution.py:15
  79.5 3.5 %copy-start.10 = (f32[512]{0:T(512)S(1)}, f32[512]{0:T(512)}, u32[]{:S(2)}) copy-start(f32[512]{0:T(512)} %param.5) | copy-start | bytes 6148
  79.5 3.6 %copy-start.9 = (s32[4,2]{0,1:T(2,128)S(1)}, s32[4,2]{0,1:T(2,128)}, u32[]{:S(2)}) copy-start(s32[4,2]{0,1:T(2,128)} %param.7) | copy-start | bytes 100
  82.8 220.4 %reduce-scatter.2.cloned.1.call-start = ((), (), s32[]{:S(2)}) async-start(), calls=%async_computation.2 | async-start | bytes 2359296 | tf_op jit(solution)/shard_map/reduce_scatter | solution.py:53
  226.8 3.8 %copy-start = (f32[512,512]{1,0:T(8,128)S(1)}, f32[512,512]{1,0:T(8,128)}, u32[]{:S(2)}) copy-start(f32[512,512]{1,0:T(8,128)} %fusion.111) | copy-start | bytes 3145732
  226.8 3.8 %copy-start.1 = (f32[512,512]{0,1:T(8,128)S(1)}, f32[512,512]{0,1:T(8,128)}, u32[]{:S(2)}) copy-start(f32[512,512]{0,1:T(8,128)} %copy.20) | copy-start | bytes 3145732
  226.8 3.8 %copy-start.2 = (f32[512,512]{1,0:T(8,128)S(1)}, f32[512,512]{1,0:T(8,128)}, u32[]{:S(2)}) copy-start(f32[512,512]{1,0:T(8,128)} %fusion.109) | copy-start | bytes 3145732
  226.8 3.8 %copy-start.3 = (f32[512,512]{0,1:T(8,128)S(1)}, f32[512,512]{0,1:T(8,128)}, u32[]{:S(2)}) copy-start(f32[512,512]{0,1:T(8,128)} %copy.19) | copy-start | bytes 3145732
  226.8 4.1 %copy-start.4 = (f32[512,512]{1,0:T(8,128)S(1)}, f32[512,512]{1,0:T(8,128)}, u32[]{:S(2)}) copy-start(f32[512,512]{1,0:T(8,128)} %fusion.105) | copy-start | bytes 3145732
  226.8 4.4 %copy-start.5 = (f32[512,512]{0,1:T(8,128)S(1)}, f32[512,512]{0,1:T(8,128)}, u32[]{:S(2)}) copy-start(f32[512,512]{0,1:T(8,128)} %copy.17) | copy-start | bytes 3145732
  226.8 4.7 %copy-start.6 = (f32[512,512]{1,0:T(8,128)S(1)}, f32[512,512]{1,0:T(8,128)}, u32[]{:S(2)}) copy-start(f32[512,512]{1,0:T(8,128)} %fusion.107) | copy-start | bytes 3145732
  226.9 4.9 %copy-start.7 = (f32[512,512]{0,1:T(8,128)S(1)}, f32[512,512]{0,1:T(8,128)}, u32[]{:S(2)}) copy-start(f32[512,512]{0,1:T(8,128)} %copy.18) | copy-start | bytes 3145732
Sparse Core Ops, SparseCore 0:
  82.9 56.5 all-gather.1
  234.5 68.7 reduce-scatter.1
